TPU v7x, 32 devices: a whole 2x2x4 slice. The times are simulated.
32 devices in a mesh: op: 4 (over y, x), str: 8 (over z, core).
Axes of the slice: x: 2, y: 2, z: 4, core: 2. Of those that a mesh axis runs over, the one named last changes fastest.
Arguments:
- coeffs: float32 [4096, 4096], P('str'), may hold values from -6 to 6
- previous: float32 [4096, 4096], P('str'), may hold values from -6 to 6
- block_values: bfloat16 [4, 32, 6, 128, 128], P('op'), may hold values from -0.21875 to 0.21875
- block_cols: int32 [4, 32, 6], P('op'), may hold values from 0 to 31, as said below
Outputs:
- advanced: float32 [4096, 4096], P('str')
Inputs may be any that keep to these rules, and one draw needn't show every extreme that they name: For every term k and block row r, block_cols[k, r, 0] equals r and the 6 entries of block_cols[k, r] are distinct.
All inputs are finite; a program needn't handle non-finite values.
Results may differ from a plain program's by a relative error of at most 0.0003.
Values sent between devices are 32-bit elements; how exact they have to be, the bound alone decides.
A program may use at most 192 MiB of HBM per device.

v0:
```python
import functools
import math

import jax
import jax.numpy as jnp
from jax import lax
from jax.experimental import pallas as pl
from jax.experimental.pallas import tpu as pltpu
from jax.sharding import PartitionSpec as P

F32, BF16 = jnp.float32, jnp.bfloat16
VMEM_LIMIT = 67_043_328


def split(x):
    high = x.astype(BF16)
    return high, (x - high.astype(F32)).astype(BF16)


def flip(a, b, size):
    total, bit = 0, 1
    while bit < size:
        total = total + bit * lax.rem(lax.div(a, bit) + lax.div(b, bit), 2)
        bit *= 2
    return total


def body(
    shards, op_size, slots, block, chunks, scale,
    cols_ref, a_hbm, v_hbm, p_hbm, out_hbm,
    a_ref, field, ysend, yrecv, wrecv, small, part, ufull, rsrecv, vstage, vq,
    a_sem, v_sem, p_sem, q_sem, o_sem,
    y_send, y_recv, r1_send, r1_recv, g1_send, g1_recv,
    w_send, w_recv, r2_send, r2_recv, g2_send, g2_recv,
):
    blocks = chunks * shards
    rows = chunks * block
    piece = rows // op_size
    thin = min(block, piece)
    wide = rows
    share = blocks // op_size
    early = max(1, chunks // 2)
    i32 = jnp.int32
    me, op = lax.axis_index("str").astype(i32), lax.axis_index("op").astype(i32)

    def peer(d):
        return flip(me, jnp.asarray(d, i32), shards)

    def mate(q):
        return flip(op, jnp.asarray(q, i32), op_size)

    def wait(ref, sem):
        pltpu.make_async_copy(ref, ref, sem).wait()

    def to_peer(src, dst, send, recv, d):
        pltpu.make_async_remote_copy(
            src_ref=src, dst_ref=dst, send_sem=send, recv_sem=recv,
            device_id={"str": peer(d)}, device_id_type=pl.DeviceIdType.MESH,
        ).start()

    def to_mate(src, dst, send, recv, q):
        pltpu.make_async_remote_copy(
            src_ref=src, dst_ref=dst, send_sem=send, recv_sem=recv,
            device_id={"op": mate(q)}, device_id_type=pl.DeviceIdType.MESH,
        ).start()

    def loop(n, start=0):
        def run(step):
            lax.fori_loop(start, n, lambda i, _: (step(i), None)[1], None)
        return run

    def v_copy(g):
        return pltpu.make_async_copy(
            v_hbm.at[:, pl.ds(pl.multiple_of(g * wide, block), wide)],
            vstage.at[lax.rem(g, 2)],
            v_sem.at[lax.rem(g, 2)],
        )

    a_copy = pltpu.make_async_copy(a_hbm, a_ref, a_sem)
    quarter = pl.ds(pl.multiple_of(op * (share * block), block), share * block)
    q_copy = pltpu.make_async_copy(v_hbm.at[:, quarter], vq, q_sem)

    v_copy(jnp.int32(0)).start()
    a_copy.start()

    barrier = pltpu.get_barrier_semaphore()
    for d in range(1, shards):
        pl.semaphore_signal(
            barrier, inc=1, device_id={"str": peer(d)}, device_id_type=pl.DeviceIdType.MESH
        )
    for q in range(1, op_size):
        pl.semaphore_signal(
            barrier, inc=1, device_id={"op": mate(q)}, device_id_type=pl.DeviceIdType.MESH
        )

    @loop(shards * chunks)
    def _(i):
        d, c = lax.div(i, chunks), lax.rem(i, chunks)
        at = pl.multiple_of((peer(d) * chunks + c) * block, block)
        pltpu.make_async_copy(
            p_hbm.at[pl.ds(pl.multiple_of(op * piece, piece), piece), pl.ds(at, block)],
            ysend.at[c, d, pl.ds(rows, piece)],
            p_sem,
        ).start()

    @loop(shards)
    def _(g):
        @pl.when(g + 1 < shards)
        def _():
            v_copy(g + 1).start()

        v_copy(g).wait()
        for i in range(chunks):
            high, low = split(vstage[lax.rem(g, 2), :, i * block : (i + 1) * block])
            field[g * chunks + i, :rows] = high
            field[g * chunks + i, rows:] = low

    q_copy.start()
    a_copy.wait()
    wait(ysend.at[:, :, pl.ds(rows, piece)], p_sem)
    pl.semaphore_wait(barrier, shards - 1 + op_size - 1)

    def operator_row(row):
        return jnp.concatenate([a_ref[row, j] for j in range(slots)], axis=1)

    def beta(source, row, m):
        left = jnp.concatenate(
            [source[cols_ref[row * slots + j]] for j in range(slots)], axis=1
        )
        both = lax.dot_general(
            left, operator_row(row), (((1,), (1,)), ((), ())), preferred_element_type=F32
        )
        return both[:m] + both[m:]

    def alpha(load, row):
        right = jnp.concatenate(
            [
                jnp.concatenate(load(cols_ref[row * slots + j]), axis=1)
                for j in range(slots)
            ],
            axis=0,
        )
        both = jnp.dot(operator_row(row), right, preferred_element_type=F32)
        return both[:, :block] + both[:, block:]

    @loop(shards * chunks)
    def _(i):
        c, d = lax.div(i, shards), lax.rem(i, shards)
        ysend[c, d, :rows] = beta(field, peer(d) * chunks + c, rows)

        @pl.when(d > 0)
        def _():
            to_peer(ysend.at[c, d], yrecv.at[c, d - 1], y_send.at[c], y_recv.at[c], d)

    def keep(at_block, x):
        high, low = split(x)
        small[at_block, :block] = high
        small[at_block, block:] = low

    def pieces(h):
        for t in range(block // thin):
            g = h * block + t * thin
            yield g // piece, g % piece, t * thin

    def alpha_first(c):
        slot = lax.rem(c, 2)
        wait(yrecv.at[c], y_recv.at[c])
        for h in range(chunks):
            keep(me * chunks + h, ysend[c, 0, h * block : (h + 1) * block])

        @loop(shards, 1)
        def _(d):
            for h in range(chunks):
                keep(peer(d) * chunks + h, yrecv[c, d - 1, h * block : (h + 1) * block])

        @pl.when(c >= 2)
        def _():
            wait(rsrecv.at[c - 2], r1_send.at[c - 2])

        @loop(shards)
        def _(d):
            for h in range(chunks):
                value = scale * alpha(
                    lambda b: [small[b, :block], small[b, block:]], peer(d) * chunks + h
                )
                for owner, at, start in pieces(h):
                    here = pl.ds(pl.multiple_of(d * piece + at, thin), thin)
                    part[slot, mate(owner), here] = value[start : start + thin]

        for q in range(1, op_size):
            to_mate(
                part.at[slot, q], rsrecv.at[c, q - 1], r1_send.at[c], r1_recv.at[c], q
            )

    def add_first(c):
        slot = lax.rem(c, 2)
        wait(rsrecv.at[c], r1_recv.at[c])

        @pl.when(c >= 2)
        def _():
            wait(ufull.at[0, pl.ds(1, op_size - 1)], g1_send.at[c - 2])

        def one(d, earlier):
            here = pl.ds(pl.multiple_of(d * piece, piece), piece)
            total = part[slot, 0, here]
            for q in range(1, op_size):
                total = total + rsrecv[c, q - 1, here]
            ufull[slot, 0, here] = total - earlier

        one(0, ysend[c, 0, rows:])

        @loop(shards, 1)
        def _(d):
            one(d, yrecv[c, d - 1, rows:])

        for q in range(1, op_size):
            to_mate(
                ufull.at[slot, 0], ufull.at[slot, q], g1_send.at[c], g1_recv.at[c], q
            )

    def alpha_piece(r, c):
        at = pl.multiple_of(r * block, block)
        column = pl.multiple_of(2 * block * c, 2 * block)

        @loop(shards)
        def _(d):
            ysend[c, d, pl.ds(at, block)] = alpha(
                lambda b: [
                    field[b, pl.ds(column, block)],
                    field[b, pl.ds(column + block, block)],
                ],
                peer(d) * chunks + r,
            )

            @pl.when(d > 0)
            def _():
                to_peer(
                    ysend.at[c, d, pl.ds(at, block)], wrecv.at[r, c, d - 1],
                    w_send.at[r], w_recv.at[r], d,
                )

    def alpha_second(c):
        slot = lax.rem(c, 2)
        wait(ufull.at[slot, pl.ds(1, op_size - 1)], g1_recv.at[c])
        column = pl.multiple_of(2 * block * c, 2 * block)

        @loop(shards)
        def _(d):
            for h in range(chunks):
                x = jnp.concatenate(
                    [
                        ufull[slot, mate(owner), pl.ds(pl.multiple_of(d * piece + at, thin), thin)]
                        for owner, at, _ in pieces(h)
                    ],
                    axis=0,
                )
                high, low = split(x)
                field[peer(d) * chunks + h, pl.ds(column, block)] = high
                field[peer(d) * chunks + h, pl.ds(column + block, block)] = low

        wait(yrecv.at[c], y_send.at[c])

        @loop(early)
        def _(r):
            alpha_piece(r, c)

    @loop(chunks + 1)
    def _(c):
        @pl.when(c < chunks)
        def _():
            alpha_first(c)

        @pl.when(c > 0)
        def _():
            alpha_second(c - 1)

        @pl.when(c < chunks)
        def _():
            add_first(c)

    for c in range(max(0, chunks - 2), chunks):
        wait(rsrecv.at[c], r1_send.at[c])
        wait(ufull.at[0, pl.ds(1, op_size - 1)], g1_send.at[c])

    @loop((chunks - early) * chunks)
    def _(i):
        alpha_piece(early + lax.div(i, chunks), lax.rem(i, chunks))

    q_copy.wait()

    def beta_second(r):
        slot = lax.rem(r, 2)
        at = pl.ds(pl.multiple_of(r * block, block), block)
        wait(wrecv.at[r], w_recv.at[r])
        for c in range(chunks):
            keep(me * chunks + c, ysend[c, 0, at])

        @loop(shards, 1)
        def _(d):
            for c in range(chunks):
                keep(peer(d) * chunks + c, wrecv[r, c, d - 1])

        @pl.when(r >= 2)
        def _():
            wait(rsrecv.at[r - 2], r2_send.at[r - 2])

        group = math.gcd(share, 4)

        @loop(blocks // group)
        def _(i):
            for g in range(group):
                b = i * group + g
                here = pl.ds(pl.multiple_of(lax.rem(b, share) * block, block), block)
                part[slot, mate(lax.div(b, share)), here] = scale * beta(small, b, block)

        for q in range(1, op_size):
            to_mate(
                part.at[slot, q], rsrecv.at[r, q - 1], r2_send.at[r], r2_recv.at[r], q
            )

    def add_second(r):
        slot = lax.rem(r, 2)
        at = pl.ds(pl.multiple_of(r * block, block), block)
        wait(rsrecv.at[r], r2_recv.at[r])
        for j in range(share):
            here, columns = pl.ds(j * block, block), pl.ds(j * block, block)
            total = part[slot, 0, here]
            for q in range(1, op_size):
                total = total + rsrecv[r, q - 1, here]
            vq[at, columns] = total - vq[at, columns]
        pltpu.make_async_copy(vq.at[at], out_hbm.at[at, quarter], o_sem.at[r]).start()
        for q in range(1, op_size):
            to_mate(vq.at[at], out_hbm.at[at, quarter], g2_send, g2_recv, q)

    @loop(chunks + 1)
    def _(r):
        @pl.when(r < chunks)
        def _():
            beta_second(r)

        @pl.when(r > 0)
        def _():
            add_second(r - 1)

    others = pl.ds(0, (op_size - 1) * share * block)
    wait(out_hbm.at[:, others], g2_recv)
    wait(out_hbm.at[:, others], g2_send)
    for r in range(chunks):
        wait(vq.at[pl.ds(r * block, block)], o_sem.at[r])
        wait(wrecv.at[r], w_send.at[r])
    for r in range(max(0, chunks - 2), chunks):
        wait(rsrecv.at[r], r2_send.at[r])


def per_device(coeffs, previous, block_values, block_cols):
    op_size, shards = lax.axis_size("op"), lax.axis_size("str")
    scale = 2.0 / math.sqrt(block_values.shape[0] * op_size)
    values = block_values[0]
    cols = block_cols[0].reshape(-1)
    blocks, slots, block, _ = values.shape
    rows, width = coeffs.shape
    chunks = blocks // shards
    piece = rows // op_size
    segment = width // op_size
    vmem, dma = pltpu.VMEM, pltpu.SemaphoreType.DMA
    anywhere = pl.BlockSpec(memory_space=pl.ANY)
    return pl.pallas_call(
        functools.partial(body, shards, op_size, slots, block, chunks, scale),
        out_shape=jax.ShapeDtypeStruct((rows, width), F32),
        in_specs=[pl.BlockSpec(memory_space=pltpu.SMEM), anywhere, anywhere, anywhere],
        out_specs=anywhere,
        scratch_shapes=[
            vmem((blocks, slots, block, block), BF16),
            vmem((blocks, 2 * rows, block), BF16),
            vmem((chunks, shards, rows + piece, block), F32),
            vmem((chunks, shards - 1, rows + piece, block), F32),
            vmem((chunks, chunks, shards - 1, block, block), F32),
            vmem((blocks, 2 * block, block), BF16),
            vmem((2, op_size, segment, block), F32),
            vmem((2, op_size, segment, block), F32),
            vmem((chunks, op_size - 1, segment, block), F32),
            vmem((2, rows, rows), F32),
            vmem((rows, segment), F32),
            dma, dma((2,)), dma, dma, dma((chunks,)),
            dma((chunks,)), dma((chunks,)), dma((chunks,)),
            dma((chunks,)), dma((chunks,)), dma((chunks,)),
            dma((chunks,)), dma((chunks,)), dma((chunks,)), dma((chunks,)),
            dma, dma,
        ],
        compiler_params=pltpu.CompilerParams(
            collective_id=0, has_side_effects=True, vmem_limit_bytes=VMEM_LIMIT
        ),
        cost_estimate=pl.CostEstimate(
            flops=16 * blocks * slots * block * block * rows,
            bytes_accessed=32 * rows * width,
            transcendentals=0,
        ),
    )(cols, values, coeffs, previous)


def solution(mesh):
    placed = (P("str", None), P("str", None), P("op", None, None, None, None), P("op", None, None))
    return jax.shard_map(
        per_device, mesh=mesh, in_specs=placed, out_specs=P("str", None), check_vma=False
    )
```

profile of v0, /device:TPU:8, one launch (start us, length us, event | category | flops | bytes accessed | tf_op | source)
XLA Modules:
  0.0 550.2 jit_solution(1635534774564742110)
XLA Ops:
  0.0 0.8 copy.5
  0.8 0.7 reshape_squeeze.3.cols_ref
  1.4 541.0 %shard_map.46 = f32[512,4096]{1,0:T(8,128)} custom-call(s32[192]{0:T(256)} %reshape_squeeze.3.cols_ref, bf16[32,6,128,128]{3,2,1,0:T(8,128)(2,1)} %bitcast.1, f32[512,4096]{1,0:T(8,128)} %v_hbm.1, f32[512,4096]{1,0:T(8,128)} %p_hbm.1), custom_call_target="tpu_custom_call" | custom-call | flops 25769803776 | bytes 67108864 | tf_op jit(solution)/shard_map/pallas_call | solution.py:367
  542.4 7.8 %copy.7 = f32[512,4096]{1,0:T(8,128)} copy(f32[512,4096]{1,0:T(8,128)} %shard_map.46) | data formatting | bytes 16777216
where the time goes:
time: 550 us
  Pallas kernels  541 us (98%)
  local copies, waits for them, and re-layouts  9.21 us (2%)
    pallas_call x1, Pallas kernels, per_device(): pl.pallas_call(functools.partial(body, shards, op_size, slots, block, chu...  541 us

commit v1 on v0

--- a/solution.py
+++ b/solution.py
@@ -28,9 +28,9 @@
 def body(
     shards, op_size, slots, block, chunks, scale,
     cols_ref, a_hbm, v_hbm, p_hbm, out_hbm,
-    a_ref, field, ysend, yrecv, wrecv, small, part, ufull, rsrecv, vstage, vq,
-    a_sem, v_sem, p_sem, q_sem, o_sem,
-    y_send, y_recv, r1_send, r1_recv, g1_send, g1_recv,
+    a_ref, field, ysend, yrecv, wrecv, precv, small, part, ufull, rsrecv, vstage, vq,
+    a_sem, v_sem, q_sem, o_sem,
+    y_send, y_recv, p_send, p_recv, r1_send, r1_recv, g1_send, g1_recv,
     w_send, w_recv, r2_send, r2_recv, g2_send, g2_recv,
 ):
     blocks = chunks * shards
@@ -39,9 +39,30 @@
     thin = min(block, piece)
     wide = rows
     share = blocks // op_size
-    early = max(1, chunks // 2)
+    segment = share * block
+    early = max(1, chunks - 1)
+    ahead = min(chunks, max(2, chunks - 2))
+    bits = max(1, op_size.bit_length() - 1)
     i32 = jnp.int32
     me, op = lax.axis_index("str").astype(i32), lax.axis_index("op").astype(i32)
+
+    def cuts(n):
+        marks = [n * p // bits // 8 * 8 for p in range(bits)] + [n]
+        return [(marks[p], marks[p + 1] - marks[p]) for p in range(bits)]
+
+    def first_bit(q, order):
+        return next(i for i, b in enumerate(order) if q >> b & 1)
+
+    orders = [[(p + i) % bits for i in range(bits)] for p in range(bits)]
+    stages = [
+        [
+            (p, q, orders[p][i])
+            for p in range(bits)
+            for q in range(1, op_size)
+            if first_bit(q, orders[p]) == i
+        ]
+        for i in range(bits)
+    ]
 
     def peer(d):
         return flip(me, jnp.asarray(d, i32), shards)
@@ -76,8 +97,15 @@
             v_sem.at[lax.rem(g, 2)],
         )
 
+    def p_part(c, d):
+        at = pl.multiple_of((peer(d) * chunks + c) * block, block)
+        return p_hbm.at[pl.ds(pl.multiple_of(op * piece, piece), piece), pl.ds(at, block)]
+
+    def send_previous(c, d):
+        to_peer(p_part(c, d), precv.at[c, d], p_send.at[c], p_recv.at[c], d)
+
     a_copy = pltpu.make_async_copy(a_hbm, a_ref, a_sem)
-    quarter = pl.ds(pl.multiple_of(op * (share * block), block), share * block)
+    quarter = pl.ds(pl.multiple_of(op * segment, block), segment)
     q_copy = pltpu.make_async_copy(v_hbm.at[:, quarter], vq, q_sem)
 
     v_copy(jnp.int32(0)).start()
@@ -93,15 +121,13 @@
             barrier, inc=1, device_id={"op": mate(q)}, device_id_type=pl.DeviceIdType.MESH
         )
 
-    @loop(shards * chunks)
-    def _(i):
-        d, c = lax.div(i, chunks), lax.rem(i, chunks)
-        at = pl.multiple_of((peer(d) * chunks + c) * block, block)
-        pltpu.make_async_copy(
-            p_hbm.at[pl.ds(pl.multiple_of(op * piece, piece), piece), pl.ds(at, block)],
-            ysend.at[c, d, pl.ds(rows, piece)],
-            p_sem,
-        ).start()
+    for c in range(chunks):
+        pltpu.make_async_copy(p_part(c, 0), precv.at[c, 0], o_sem.at[c]).start()
+    pl.semaphore_wait(barrier, shards - 1 + op_size - 1)
+
+    @loop(shards, 1)
+    def _(d):
+        send_previous(0, d)
 
     @loop(shards)
     def _(g):
@@ -115,10 +141,9 @@
             field[g * chunks + i, :rows] = high
             field[g * chunks + i, rows:] = low
 
-    q_copy.start()
     a_copy.wait()
-    wait(ysend.at[:, :, pl.ds(rows, piece)], p_sem)
-    pl.semaphore_wait(barrier, shards - 1 + op_size - 1)
+    for c in range(chunks):
+        wait(precv.at[c, 0], o_sem.at[c])
 
     def operator_row(row):
         return jnp.concatenate([a_ref[row, j] for j in range(slots)], axis=1)
@@ -143,14 +168,66 @@
         both = jnp.dot(operator_row(row), right, preferred_element_type=F32)
         return both[:, :block] + both[:, block:]
 
-    @loop(shards * chunks)
-    def _(i):
-        c, d = lax.div(i, shards), lax.rem(i, shards)
-        ysend[c, d, :rows] = beta(field, peer(d) * chunks + c, rows)
-
-        @pl.when(d > 0)
-        def _():
-            to_peer(ysend.at[c, d], yrecv.at[c, d - 1], y_send.at[c], y_recv.at[c], d)
+    def send_stage(slot, c, stage, send, recv):
+        for p, q, b in stages[stage]:
+            lo, n = cuts(segment)[p]
+            to_mate(
+                part.at[slot, q, pl.ds(lo, n)], rsrecv.at[c, q - 1, pl.ds(lo, n)],
+                send.at[c, q - 1, p], recv.at[c, q - 1, p], 1 << b,
+            )
+
+    def arrived(c, stage, recv):
+        for p, q, b in stages[stage]:
+            lo, n = cuts(segment)[p]
+            wait(rsrecv.at[c, q - 1, pl.ds(lo, n)], recv.at[c, q - 1, p])
+
+    def relay_stages(slot, c, send, recv):
+        for stage in range(bits - 1):
+            arrived(c, stage, recv)
+            for p, q, b in stages[stage]:
+                left = q ^ (1 << b)
+                if left:
+                    lo, n = cuts(segment)[p]
+                    here = pl.ds(lo, n)
+                    part[slot, left, here] = part[slot, left, here] + rsrecv[c, q - 1, here]
+            send_stage(slot, c, stage + 1, send, recv)
+
+    def sum_sent(c, send):
+        for p in range(bits):
+            lo, n = cuts(segment)[p]
+            for q in range(1, op_size):
+                wait(rsrecv.at[c, q - 1, pl.ds(lo, n)], send.at[c, q - 1, p])
+
+    def own_total(slot, c, at, n):
+        here = pl.ds(at, n)
+        total = part[slot, 0, here]
+        for b in range(bits):
+            total = total + rsrecv[c, (1 << b) - 1, here]
+        return total
+
+    def hand_out(c, copy, have):
+        for p in range(bits):
+            order = orders[p][::-1]
+            for q in range(1, op_size):
+                last = max(i for i, b in enumerate(order) if q >> b & 1)
+                source = q ^ (1 << order[last])
+                if source in have:
+                    copy(c, p, source, q, 1 << order[last])
+
+    waves = [[q for q in range(op_size) if bin(q).count("1") == n] for n in range(bits + 1)]
+
+    def beta_first(c):
+        @loop(shards)
+        def _(d):
+            ysend[c, d] = beta(field, peer(d) * chunks + c, rows)
+
+            @pl.when(d > 0)
+            def _():
+                to_peer(ysend.at[c, d], yrecv.at[c, d - 1], y_send.at[c], y_recv.at[c], d)
+
+                @pl.when(c + 1 < chunks)
+                def _():
+                    send_previous(c + 1, d)
 
     def keep(at_block, x):
         high, low = split(x)
@@ -175,7 +252,8 @@
 
         @pl.when(c >= 2)
         def _():
-            wait(rsrecv.at[c - 2], r1_send.at[c - 2])
+            sum_sent(c - 2, r1_send)
+            handed_first(c - 2, g1_send, range(1, op_size))
 
         @loop(shards)
         def _(d):
@@ -187,36 +265,39 @@
                     here = pl.ds(pl.multiple_of(d * piece + at, thin), thin)
                     part[slot, mate(owner), here] = value[start : start + thin]
 
-        for q in range(1, op_size):
-            to_mate(
-                part.at[slot, q], rsrecv.at[c, q - 1], r1_send.at[c], r1_recv.at[c], q
-            )
+        send_stage(slot, c, 0, r1_send, r1_recv)
+
+    def hand_first(c, p, source, q, across):
+        slot = lax.rem(c, 2)
+        lo, n = cuts(segment)[p]
+        to_mate(
+            ufull.at[slot, source, pl.ds(lo, n)], ufull.at[slot, q, pl.ds(lo, n)],
+            g1_send.at[c, q - 1, p], g1_recv.at[c, q - 1, p], across,
+        )
+
+    def handed_first(c, sem, slots_):
+        for p in range(bits):
+            lo, n = cuts(segment)[p]
+            for q in slots_:
+                wait(ufull.at[lax.rem(c, 2), q, pl.ds(lo, n)], sem.at[c, q - 1, p])
 
     def add_first(c):
         slot = lax.rem(c, 2)
-        wait(rsrecv.at[c], r1_recv.at[c])
-
-        @pl.when(c >= 2)
-        def _():
-            wait(ufull.at[0, pl.ds(1, op_size - 1)], g1_send.at[c - 2])
-
-        def one(d, earlier):
-            here = pl.ds(pl.multiple_of(d * piece, piece), piece)
-            total = part[slot, 0, here]
-            for q in range(1, op_size):
-                total = total + rsrecv[c, q - 1, here]
-            ufull[slot, 0, here] = total - earlier
-
-        one(0, ysend[c, 0, rows:])
-
-        @loop(shards, 1)
-        def _(d):
-            one(d, yrecv[c, d - 1, rows:])
-
-        for q in range(1, op_size):
-            to_mate(
-                ufull.at[slot, 0], ufull.at[slot, q], g1_send.at[c], g1_recv.at[c], q
-            )
+        relay_stages(slot, c, r1_send, r1_recv)
+
+        @pl.when(c == 0)
+        def _():
+            q_copy.start()
+
+        wait(precv.at[c, pl.ds(1, shards - 1)], p_recv.at[c])
+        arrived(c, bits - 1, r1_recv)
+
+        @loop(shards)
+        def _(d):
+            at = pl.multiple_of(d * piece, piece)
+            ufull[slot, 0, pl.ds(at, piece)] = own_total(slot, c, at, piece) - precv[c, d]
+
+        hand_out(c, hand_first, waves[0])
 
     def alpha_piece(r, c):
         at = pl.multiple_of(r * block, block)
@@ -241,7 +322,9 @@
 
     def alpha_second(c):
         slot = lax.rem(c, 2)
-        wait(ufull.at[slot, pl.ds(1, op_size - 1)], g1_recv.at[c])
+        for wave in waves[1:]:
+            handed_first(c, g1_recv, wave)
+            hand_out(c, hand_first, wave)
         column = pl.multiple_of(2 * block * c, 2 * block)
 
         @loop(shards)
@@ -264,12 +347,20 @@
         def _(r):
             alpha_piece(r, c)
 
+    @loop(ahead)
+    def _(c):
+        beta_first(c)
+
     @loop(chunks + 1)
     def _(c):
         @pl.when(c < chunks)
         def _():
             alpha_first(c)
 
+        @pl.when(c + ahead < chunks)
+        def _():
+            beta_first(c + ahead)
+
         @pl.when(c > 0)
         def _():
             alpha_second(c - 1)
@@ -277,20 +368,22 @@
         @pl.when(c < chunks)
         def _():
             add_first(c)
-
-    for c in range(max(0, chunks - 2), chunks):
-        wait(rsrecv.at[c], r1_send.at[c])
-        wait(ufull.at[0, pl.ds(1, op_size - 1)], g1_send.at[c])
 
     @loop((chunks - early) * chunks)
     def _(i):
         alpha_piece(early + lax.div(i, chunks), lax.rem(i, chunks))
 
+    for c in range(max(0, chunks - 2), chunks):
+        sum_sent(c, r1_send)
+        handed_first(c, g1_send, range(1, op_size))
     q_copy.wait()
+
+    def row_block(r):
+        return pl.ds(pl.multiple_of(r * block, block), block)
 
     def beta_second(r):
         slot = lax.rem(r, 2)
-        at = pl.ds(pl.multiple_of(r * block, block), block)
+        at = row_block(r)
         wait(wrecv.at[r], w_recv.at[r])
         for c in range(chunks):
             keep(me * chunks + c, ysend[c, 0, at])
@@ -302,7 +395,7 @@
 
         @pl.when(r >= 2)
         def _():
-            wait(rsrecv.at[r - 2], r2_send.at[r - 2])
+            sum_sent(r - 2, r2_send)
 
         group = math.gcd(share, 4)
 
@@ -313,43 +406,64 @@
                 here = pl.ds(pl.multiple_of(lax.rem(b, share) * block, block), block)
                 part[slot, mate(lax.div(b, share)), here] = scale * beta(small, b, block)
 
-        for q in range(1, op_size):
-            to_mate(
-                part.at[slot, q], rsrecv.at[r, q - 1], r2_send.at[r], r2_recv.at[r], q
-            )
+        send_stage(slot, r, 0, r2_send, r2_recv)
+
+    def out_part(r, p, q):
+        lo, n = cuts(block)[p]
+        here = pl.ds(pl.multiple_of(r * block + lo, 8), n)
+        return out_hbm.at[here, pl.ds(pl.multiple_of(mate(q) * segment, segment), segment)]
+
+    def hand_second(r, p, source, q, across):
+        lo, n = cuts(block)[p]
+        own = vq.at[pl.ds(pl.multiple_of(r * block + lo, 8), n)]
+        there = out_part(r, p, source)
+        to_mate(
+            there if source else own, there,
+            g2_send.at[r, q - 1, p], g2_recv.at[r, q - 1, p], across,
+        )
 
     def add_second(r):
         slot = lax.rem(r, 2)
-        at = pl.ds(pl.multiple_of(r * block, block), block)
-        wait(rsrecv.at[r], r2_recv.at[r])
+        at = row_block(r)
+        arrived(r, bits - 1, r2_recv)
         for j in range(share):
-            here, columns = pl.ds(j * block, block), pl.ds(j * block, block)
-            total = part[slot, 0, here]
-            for q in range(1, op_size):
-                total = total + rsrecv[r, q - 1, here]
-            vq[at, columns] = total - vq[at, columns]
+            columns = pl.ds(j * block, block)
+            vq[at, columns] = own_total(slot, r, j * block, block) - vq[at, columns]
+        hand_out(r, hand_second, waves[0])
         pltpu.make_async_copy(vq.at[at], out_hbm.at[at, quarter], o_sem.at[r]).start()
-        for q in range(1, op_size):
-            to_mate(vq.at[at], out_hbm.at[at, quarter], g2_send, g2_recv, q)
-
-    @loop(chunks + 1)
-    def _(r):
-        @pl.when(r < chunks)
-        def _():
-            beta_second(r)
-
-        @pl.when(r > 0)
-        def _():
-            add_second(r - 1)
-
-    others = pl.ds(0, (op_size - 1) * share * block)
-    wait(out_hbm.at[:, others], g2_recv)
-    wait(out_hbm.at[:, others], g2_send)
+
+    def handed_second(r, sem, slots_):
+        for p in range(bits):
+            for q in slots_:
+                wait(out_part(r, p, q), sem.at[r, q - 1, p])
+
+    def relay_second(r):
+        for wave in waves[1:]:
+            handed_second(r, g2_recv, wave)
+            hand_out(r, hand_second, wave)
+
+    def at_tick(t, act):
+        last = chunks + 1
+        early_one = jnp.logical_and(t >= 0, t < chunks - 1)
+
+        @pl.when(jnp.logical_or(early_one, t == last))
+        def _():
+            act(jnp.minimum(t, chunks - 1))
+
+    @loop(chunks + 5)
+    def _(t):
+        at_tick(t - 3, relay_second)
+        at_tick(t - 2, add_second)
+        at_tick(t, beta_second)
+        at_tick(t - 1, lambda r: relay_stages(lax.rem(r, 2), r, r2_send, r2_recv))
+
     for r in range(chunks):
+        handed_second(r, g2_send, range(1, op_size))
         wait(vq.at[pl.ds(r * block, block)], o_sem.at[r])
         wait(wrecv.at[r], w_send.at[r])
+        wait(precv.at[r, pl.ds(1, shards - 1)], p_send.at[r])
     for r in range(max(0, chunks - 2), chunks):
-        wait(rsrecv.at[r], r2_send.at[r])
+        sum_sent(r, r2_send)
 
 
 def per_device(coeffs, previous, block_values, block_cols):
@@ -362,6 +476,7 @@
     chunks = blocks // shards
     piece = rows // op_size
     segment = width // op_size
+    paths = (chunks, op_size - 1, max(1, op_size.bit_length() - 1))
     vmem, dma = pltpu.VMEM, pltpu.SemaphoreType.DMA
     anywhere = pl.BlockSpec(memory_space=pl.ANY)
     return pl.pallas_call(
@@ -372,20 +487,21 @@
         scratch_shapes=[
             vmem((blocks, slots, block, block), BF16),
             vmem((blocks, 2 * rows, block), BF16),
-            vmem((chunks, shards, rows + piece, block), F32),
-            vmem((chunks, shards - 1, rows + piece, block), F32),
+            vmem((chunks, shards, rows, block), F32),
+            vmem((chunks, shards - 1, rows, block), F32),
             vmem((chunks, chunks, shards - 1, block, block), F32),
+            vmem((chunks, shards, piece, block), F32),
             vmem((blocks, 2 * block, block), BF16),
             vmem((2, op_size, segment, block), F32),
             vmem((2, op_size, segment, block), F32),
             vmem((chunks, op_size - 1, segment, block), F32),
             vmem((2, rows, rows), F32),
             vmem((rows, segment), F32),
-            dma, dma((2,)), dma, dma, dma((chunks,)),
-            dma((chunks,)), dma((chunks,)), dma((chunks,)),
-            dma((chunks,)), dma((chunks,)), dma((chunks,)),
+            dma, dma((2,)), dma, dma((chunks,)),
             dma((chunks,)), dma((chunks,)), dma((chunks,)), dma((chunks,)),
-            dma, dma,
+            dma(paths), dma(paths), dma(paths), dma(paths),
+            dma((chunks,)), dma((chunks,)),
+            dma(paths), dma(paths), dma(paths), dma(paths),
         ],
         compiler_params=pltpu.CompilerParams(
             collective_id=0, has_side_effects=True, vmem_limit_bytes=VMEM_LIMIT

time: 550 us -> 544 us (0.989)
  Pallas kernels: 541 us -> 535 us
    pallas_call x1, Pallas kernels: 541 us -> 535 us  [per_device(): pl.pallas_call(functools.partial(body, shards, op_size, slots, block, chu...]
where the time goes in v1:
time: 544 us
  Pallas kernels  535 us (98%)
  local copies, waits for them, and re-layouts  9.21 us (2%)
    pallas_call x1, Pallas kernels, per_device(): pl.pallas_call(functools.partial(body, shards, op_size, slots, block, chu...  535 us

profile of v1, /device:TPU:8, one launch (start us, length us, event | category | flops | bytes accessed | tf_op | source)
XLA Modules:
  0.0 544.1 jit_solution(9023667716637578093)
XLA Ops:
  0.0 0.8 copy.5
  0.8 0.7 reshape_squeeze.3.cols_ref
  1.4 534.8 %shard_map.46 = f32[512,4096]{1,0:T(8,128)} custom-call(s32[192]{0:T(256)} %reshape_squeeze.3.cols_ref, bf16[32,6,128,128]{3,2,1,0:T(8,128)(2,1)} %bitcast.1, f32[512,4096]{1,0:T(8,128)} %v_hbm.1, f32[512,4096]{1,0:T(8,128)} %p_hbm.1), custom_call_target="tpu_custom_call" | custom-call | flops 25769803776 | bytes 67108864 | tf_op jit(solution)/shard_map/pallas_call | solution.py:482
  536.3 7.8 %copy.7 = f32[512,4096]{1,0:T(8,128)} copy(f32[512,4096]{1,0:T(8,128)} %shard_map.46) | data formatting | bytes 16777216

commit v2 on v1

--- a/solution.py
+++ b/solution.py
@@ -40,8 +40,8 @@
     wide = rows
     share = blocks // op_size
     segment = share * block
-    early = max(1, chunks - 1)
-    ahead = min(chunks, max(2, chunks - 2))
+    early = max(1, chunks // 2)
+    near = max(1, shards // 2)
     bits = max(1, op_size.bit_length() - 1)
     i32 = jnp.int32
     me, op = lax.axis_index("str").astype(i32), lax.axis_index("op").astype(i32)
@@ -172,37 +172,37 @@
         for p, q, b in stages[stage]:
             lo, n = cuts(segment)[p]
             to_mate(
-                part.at[slot, q, pl.ds(lo, n)], rsrecv.at[c, q - 1, pl.ds(lo, n)],
+                part.at[slot, q, pl.ds(lo, n)], rsrecv.at[slot, q - 1, pl.ds(lo, n)],
                 send.at[c, q - 1, p], recv.at[c, q - 1, p], 1 << b,
             )
 
-    def arrived(c, stage, recv):
+    def arrived(slot, c, stage, recv):
         for p, q, b in stages[stage]:
             lo, n = cuts(segment)[p]
-            wait(rsrecv.at[c, q - 1, pl.ds(lo, n)], recv.at[c, q - 1, p])
+            wait(rsrecv.at[slot, q - 1, pl.ds(lo, n)], recv.at[c, q - 1, p])
 
     def relay_stages(slot, c, send, recv):
         for stage in range(bits - 1):
-            arrived(c, stage, recv)
+            arrived(slot, c, stage, recv)
             for p, q, b in stages[stage]:
                 left = q ^ (1 << b)
                 if left:
                     lo, n = cuts(segment)[p]
                     here = pl.ds(lo, n)
-                    part[slot, left, here] = part[slot, left, here] + rsrecv[c, q - 1, here]
+                    part[slot, left, here] = part[slot, left, here] + rsrecv[slot, q - 1, here]
             send_stage(slot, c, stage + 1, send, recv)
 
     def sum_sent(c, send):
         for p in range(bits):
             lo, n = cuts(segment)[p]
             for q in range(1, op_size):
-                wait(rsrecv.at[c, q - 1, pl.ds(lo, n)], send.at[c, q - 1, p])
-
-    def own_total(slot, c, at, n):
+                wait(rsrecv.at[0, q - 1, pl.ds(lo, n)], send.at[c, q - 1, p])
+
+    def own_total(slot, at, n):
         here = pl.ds(at, n)
         total = part[slot, 0, here]
         for b in range(bits):
-            total = total + rsrecv[c, (1 << b) - 1, here]
+            total = total + rsrecv[slot, (1 << b) - 1, here]
         return total
 
     def hand_out(c, copy, have):
@@ -216,8 +216,8 @@
 
     waves = [[q for q in range(op_size) if bin(q).count("1") == n] for n in range(bits + 1)]
 
-    def beta_first(c):
-        @loop(shards)
+    def beta_first(c, start, end):
+        @loop(end, start)
         def _(d):
             ysend[c, d] = beta(field, peer(d) * chunks + c, rows)
 
@@ -241,7 +241,6 @@
 
     def alpha_first(c):
         slot = lax.rem(c, 2)
-        wait(yrecv.at[c], y_recv.at[c])
         for h in range(chunks):
             keep(me * chunks + h, ysend[c, 0, h * block : (h + 1) * block])
 
@@ -253,7 +252,6 @@
         @pl.when(c >= 2)
         def _():
             sum_sent(c - 2, r1_send)
-            handed_first(c - 2, g1_send, range(1, op_size))
 
         @loop(shards)
         def _(d):
@@ -268,10 +266,9 @@
         send_stage(slot, c, 0, r1_send, r1_recv)
 
     def hand_first(c, p, source, q, across):
-        slot = lax.rem(c, 2)
         lo, n = cuts(segment)[p]
         to_mate(
-            ufull.at[slot, source, pl.ds(lo, n)], ufull.at[slot, q, pl.ds(lo, n)],
+            ufull.at[c, source, pl.ds(lo, n)], ufull.at[c, q, pl.ds(lo, n)],
             g1_send.at[c, q - 1, p], g1_recv.at[c, q - 1, p], across,
         )
 
@@ -279,7 +276,7 @@
         for p in range(bits):
             lo, n = cuts(segment)[p]
             for q in slots_:
-                wait(ufull.at[lax.rem(c, 2), q, pl.ds(lo, n)], sem.at[c, q - 1, p])
+                wait(ufull.at[c, q, pl.ds(lo, n)], sem.at[c, q - 1, p])
 
     def add_first(c):
         slot = lax.rem(c, 2)
@@ -290,12 +287,12 @@
             q_copy.start()
 
         wait(precv.at[c, pl.ds(1, shards - 1)], p_recv.at[c])
-        arrived(c, bits - 1, r1_recv)
+        arrived(slot, c, bits - 1, r1_recv)
 
         @loop(shards)
         def _(d):
             at = pl.multiple_of(d * piece, piece)
-            ufull[slot, 0, pl.ds(at, piece)] = own_total(slot, c, at, piece) - precv[c, d]
+            ufull[c, 0, pl.ds(at, piece)] = own_total(slot, at, piece) - precv[c, d]
 
         hand_out(c, hand_first, waves[0])
 
@@ -320,11 +317,13 @@
                     w_send.at[r], w_recv.at[r], d,
                 )
 
-    def alpha_second(c):
-        slot = lax.rem(c, 2)
-        for wave in waves[1:]:
+    def relay_first(c):
+        for wave in waves[1:-1]:
             handed_first(c, g1_recv, wave)
             hand_out(c, hand_first, wave)
+
+    def alpha_second(c):
+        handed_first(c, g1_recv, waves[-1])
         column = pl.multiple_of(2 * block * c, 2 * block)
 
         @loop(shards)
@@ -332,7 +331,7 @@
             for h in range(chunks):
                 x = jnp.concatenate(
                     [
-                        ufull[slot, mate(owner), pl.ds(pl.multiple_of(d * piece + at, thin), thin)]
+                        ufull[c, mate(owner), pl.ds(pl.multiple_of(d * piece + at, thin), thin)]
                         for owner, at, _ in pieces(h)
                     ],
                     axis=0,
@@ -347,27 +346,32 @@
         def _(r):
             alpha_piece(r, c)
 
-    @loop(ahead)
+    beta_first(0, 0, shards)
+    if chunks > 1:
+        beta_first(1, 0, near)
+
+    @loop(chunks)
     def _(c):
-        beta_first(c)
-
-    @loop(chunks + 1)
-    def _(c):
-        @pl.when(c < chunks)
-        def _():
-            alpha_first(c)
-
-        @pl.when(c + ahead < chunks)
-        def _():
-            beta_first(c + ahead)
-
-        @pl.when(c > 0)
-        def _():
-            alpha_second(c - 1)
-
-        @pl.when(c < chunks)
-        def _():
-            add_first(c)
+        wait(yrecv.at[c], y_recv.at[c])
+
+        @pl.when(c + 1 < chunks)
+        def _():
+            beta_first(c + 1, near, shards)
+
+        @pl.when(c + 2 < chunks)
+        def _():
+            beta_first(c + 2, 0, near)
+
+        alpha_first(c)
+
+        @pl.when(c == chunks - 1)
+        def _():
+            loop(chunks - 1)(alpha_second)
+
+        add_first(c)
+        relay_first(c)
+
+    alpha_second(chunks - 1)
 
     @loop((chunks - early) * chunks)
     def _(i):
@@ -375,6 +379,7 @@
 
     for c in range(max(0, chunks - 2), chunks):
         sum_sent(c, r1_send)
+    for c in range(chunks):
         handed_first(c, g1_send, range(1, op_size))
     q_copy.wait()
 
@@ -425,10 +430,10 @@
     def add_second(r):
         slot = lax.rem(r, 2)
         at = row_block(r)
-        arrived(r, bits - 1, r2_recv)
+        arrived(slot, r, bits - 1, r2_recv)
         for j in range(share):
             columns = pl.ds(j * block, block)
-            vq[at, columns] = own_total(slot, r, j * block, block) - vq[at, columns]
+            vq[at, columns] = own_total(slot, j * block, block) - vq[at, columns]
         hand_out(r, hand_second, waves[0])
         pltpu.make_async_copy(vq.at[at], out_hbm.at[at, quarter], o_sem.at[r]).start()
 
@@ -442,20 +447,29 @@
             handed_second(r, g2_recv, wave)
             hand_out(r, hand_second, wave)
 
-    def at_tick(t, act):
-        last = chunks + 1
-        early_one = jnp.logical_and(t >= 0, t < chunks - 1)
-
-        @pl.when(jnp.logical_or(early_one, t == last))
-        def _():
-            act(jnp.minimum(t, chunks - 1))
-
-    @loop(chunks + 5)
+    acts = {
+        "beta": beta_second,
+        "relay": lambda r: relay_stages(lax.rem(r, 2), r, r2_send, r2_recv),
+        "add": add_second,
+        "hand": relay_second,
+    }
+    pair = range(min(2, chunks))
+    order = [(act, r) for act in ("beta", "relay", "add", "hand") for r in pair]
+    for r in range(2, chunks):
+        at = len(order) - 1 if r == 2 else len(order)
+        order.insert(at, ("beta", r))
+        order += [(act, r) for act in ("relay", "add", "hand")]
+
+    @loop(len(order))
     def _(t):
-        at_tick(t - 3, relay_second)
-        at_tick(t - 2, add_second)
-        at_tick(t, beta_second)
-        at_tick(t - 1, lambda r: relay_stages(lax.rem(r, 2), r, r2_send, r2_recv))
+        for name, act in acts.items():
+            ticks = [order.index((name, r)) for r in range(chunks)]
+            now = functools.reduce(jnp.logical_or, [t == k for k in ticks])
+            r = sum(jnp.minimum(jnp.maximum(t - k + 1, 0), 1) for k in ticks) - 1
+
+            @pl.when(now)
+            def _():
+                act(r)
 
     for r in range(chunks):
         handed_second(r, g2_send, range(1, op_size))
@@ -493,8 +507,8 @@
             vmem((chunks, shards, piece, block), F32),
             vmem((blocks, 2 * block, block), BF16),
             vmem((2, op_size, segment, block), F32),
-            vmem((2, op_size, segment, block), F32),
-            vmem((chunks, op_size - 1, segment, block), F32),
+            vmem((chunks, op_size, segment, block), F32),
+            vmem((2, op_size - 1, segment, block), F32),
             vmem((2, rows, rows), F32),
             vmem((rows, segment), F32),
             dma, dma((2,)), dma, dma((chunks,)),

time: 544 us -> 539 us (level)
  Pallas kernels: 535 us -> 529 us
where the time goes in v2:
time: 539 us
  Pallas kernels  529 us (98%)
  local copies, waits for them, and re-layouts  9.21 us (2%)
    pallas_call x1, Pallas kernels, per_device(): pl.pallas_call(functools.partial(body, shards, op_size, slots, block, chu...  529 us

profile of v2, /device:TPU:8, one launch (start us, length us, event | category | flops | bytes accessed | tf_op | source)
XLA Modules:
  0.0 538.6 jit_solution(6003030346433383027)
XLA Ops:
  0.0 0.8 copy.5
  0.8 0.7 reshape_squeeze.3.cols_ref
  1.4 529.4 %shard_map.46 = f32[512,4096]{1,0:T(8,128)} custom-call(s32[192]{0:T(256)} %reshape_squeeze.3.cols_ref, bf16[32,6,128,128]{3,2,1,0:T(8,128)(2,1)} %bitcast.1, f32[512,4096]{1,0:T(8,128)} %v_hbm.1, f32[512,4096]{1,0:T(8,128)} %p_hbm.1), custom_call_target="tpu_custom_call" | custom-call | flops 25769803776 | bytes 67108864 | tf_op jit(solution)/shard_map/pallas_call | solution.py:496
  530.9 7.8 %copy.7 = f32[512,4096]{1,0:T(8,128)} copy(f32[512,4096]{1,0:T(8,128)} %shard_map.46) | data formatting | bytes 16777216

commit v3 on v2

--- a/solution.py
+++ b/solution.py
@@ -296,11 +296,11 @@
 
         hand_out(c, hand_first, waves[0])
 
-    def alpha_piece(r, c):
+    def alpha_piece(r, c, start, end):
         at = pl.multiple_of(r * block, block)
         column = pl.multiple_of(2 * block * c, 2 * block)
 
-        @loop(shards)
+        @loop(end, start)
         def _(d):
             ysend[c, d, pl.ds(at, block)] = alpha(
                 lambda b: [
@@ -344,7 +344,7 @@
 
         @loop(early)
         def _(r):
-            alpha_piece(r, c)
+            alpha_piece(r, c, 0, shards)
 
     beta_first(0, 0, shards)
     if chunks > 1:
@@ -375,7 +375,10 @@
 
     @loop((chunks - early) * chunks)
     def _(i):
-        alpha_piece(early + lax.div(i, chunks), lax.rem(i, chunks))
+        alpha_piece(early + lax.div(i, chunks), lax.rem(i, chunks), 0, near)
+
+    def send_far(r):
+        loop(chunks)(lambda c: alpha_piece(r, c, near, shards))
 
     for c in range(max(0, chunks - 2), chunks):
         sum_sent(c, r1_send)
@@ -390,6 +393,11 @@
         slot = lax.rem(r, 2)
         at = row_block(r)
         wait(wrecv.at[r], w_recv.at[r])
+
+        @pl.when(jnp.logical_and(r >= early, r + 1 < chunks))
+        def _():
+            send_far(r + 1)
+
         for c in range(chunks):
             keep(me * chunks + c, ysend[c, 0, at])
 
@@ -412,6 +420,12 @@
                 part[slot, mate(lax.div(b, share)), here] = scale * beta(small, b, block)
 
         send_stage(slot, r, 0, r2_send, r2_recv)
+
+        @pl.when(r == 0)
+        def _():
+            if early < chunks:
+                send_far(early)
+
 
     def out_part(r, p, q):
         lo, n = cuts(block)[p]
@@ -456,7 +470,7 @@
     pair = range(min(2, chunks))
     order = [(act, r) for act in ("beta", "relay", "add", "hand") for r in pair]
     for r in range(2, chunks):
-        at = len(order) - 1 if r == 2 else len(order)
+        at = len(order) - 1
         order.insert(at, ("beta", r))
         order += [(act, r) for act in ("relay", "add", "hand")]
 

time: 539 us -> 505 us (0.937)
  Pallas kernels: 529 us -> 496 us
    pallas_call x1, Pallas kernels: 529 us -> 496 us  [per_device(): pl.pallas_call(functools.partial(body, shards, op_size, slots, block, chu...]
where the time goes in v3:
time: 505 us
  Pallas kernels  496 us (98%)
  local copies, waits for them, and re-layouts  9.21 us (2%)
    pallas_call x1, Pallas kernels, per_device(): pl.pallas_call(functools.partial(body, shards, op_size, slots, block, chu...  496 us

profile of v3, /device:TPU:8, one launch (start us, length us, event | category | flops | bytes accessed | tf_op | source)
XLA Modules:
  0.0 505.2 jit_solution(8029667017410844613)
XLA Ops:
  0.0 0.8 copy.5
  0.8 0.7 reshape_squeeze.3.cols_ref
  1.4 495.9 %shard_map.46 = f32[512,4096]{1,0:T(8,128)} custom-call(s32[192]{0:T(256)} %reshape_squeeze.3.cols_ref, bf16[32,6,128,128]{3,2,1,0:T(8,128)(2,1)} %bitcast.1, f32[512,4096]{1,0:T(8,128)} %v_hbm.1, f32[512,4096]{1,0:T(8,128)} %p_hbm.1), custom_call_target="tpu_custom_call" | custom-call | flops 25769803776 | bytes 67108864 | tf_op jit(solution)/shard_map/pallas_call | solution.py:510
  497.4 7.8 %copy.7 = f32[512,4096]{1,0:T(8,128)} copy(f32[512,4096]{1,0:T(8,128)} %shard_map.46) | data formatting | bytes 16777216

commit v4 on v3

--- a/solution.py
+++ b/solution.py
@@ -377,8 +377,13 @@
     def _(i):
         alpha_piece(early + lax.div(i, chunks), lax.rem(i, chunks), 0, near)
 
-    def send_far(r):
-        loop(chunks)(lambda c: alpha_piece(r, c, near, shards))
+    half = chunks // 2
+
+    def send_far(r, start, end):
+        loop(end, start)(lambda c: alpha_piece(r, c, near, shards))
+
+    if early < chunks:
+        send_far(early, 0, half)
 
     for c in range(max(0, chunks - 2), chunks):
         sum_sent(c, r1_send)
@@ -396,7 +401,12 @@
 
         @pl.when(jnp.logical_and(r >= early, r + 1 < chunks))
         def _():
-            send_far(r + 1)
+            send_far(r + 1, half, chunks)
+
+        if early + 2 < chunks:
+            @pl.when(jnp.logical_and(r >= early, r + 2 < chunks))
+            def _():
+                send_far(r + 2, 0, half)
 
         for c in range(chunks):
             keep(me * chunks + c, ysend[c, 0, at])
@@ -424,7 +434,9 @@
         @pl.when(r == 0)
         def _():
             if early < chunks:
-                send_far(early)
+                send_far(early, half, chunks)
+            if early + 1 < chunks:
+                send_far(early + 1, 0, half)
 
 
     def out_part(r, p, q):
@@ -457,7 +469,7 @@
                 wait(out_part(r, p, q), sem.at[r, q - 1, p])
 
     def relay_second(r):
-        for wave in waves[1:]:
+        for wave in waves[1:-1]:
             handed_second(r, g2_recv, wave)
             hand_out(r, hand_second, wave)
 
@@ -467,11 +479,10 @@
         "add": add_second,
         "hand": relay_second,
     }
-    pair = range(min(2, chunks))
-    order = [(act, r) for act in ("beta", "relay", "add", "hand") for r in pair]
+    order = [(act, r) for r in range(min(2, chunks)) for act in ("beta", "relay")]
+    order += [(act, r) for act in ("add", "hand") for r in range(min(2, chunks))]
     for r in range(2, chunks):
-        at = len(order) - 1
-        order.insert(at, ("beta", r))
+        order.insert(len(order) - (r == 2), ("beta", r))
         order += [(act, r) for act in ("relay", "add", "hand")]
 
     @loop(len(order))
@@ -486,6 +497,7 @@
                 act(r)
 
     for r in range(chunks):
+        handed_second(r, g2_recv, waves[-1])
         handed_second(r, g2_send, range(1, op_size))
         wait(vq.at[pl.ds(r * block, block)], o_sem.at[r])
         wait(wrecv.at[r], w_send.at[r])

time: 505 us -> 517 us (1.024)
  Pallas kernels: 496 us -> 507 us
    pallas_call x1, Pallas kernels: 496 us -> 507 us  [per_device(): pl.pallas_call(functools.partial(body, shards, op_size, slots, block, chu...]
where the time goes in v4:
time: 517 us; the launch traced here: 516 us
  Pallas kernels  507 us (98%)
  local copies, waits for them, and re-layouts  9.21 us (2%)
    pallas_call x1, Pallas kernels, per_device(): pl.pallas_call(functools.partial(body, shards, op_size, slots, block, chu...  507 us

profile of v4, /device:TPU:8, one launch (start us, length us, event | category | flops | bytes accessed | tf_op | source)
XLA Modules:
  0.0 516.4 jit_solution(9176407962633022397)
XLA Ops:
  0.0 0.8 copy.5
  0.8 0.7 reshape_squeeze.3.cols_ref
  1.4 507.2 %shard_map.46 = f32[512,4096]{1,0:T(8,128)} custom-call(s32[192]{0:T(256)} %reshape_squeeze.3.cols_ref, bf16[32,6,128,128]{3,2,1,0:T(8,128)(2,1)} %bitcast.1, f32[512,4096]{1,0:T(8,128)} %v_hbm.1, f32[512,4096]{1,0:T(8,128)} %p_hbm.1), custom_call_target="tpu_custom_call" | custom-call | flops 25769803776 | bytes 67108864 | tf_op jit(solution)/shard_map/pallas_call | solution.py:522
  508.6 7.8 %copy.7 = f32[512,4096]{1,0:T(8,128)} copy(f32[512,4096]{1,0:T(8,128)} %shard_map.46) | data formatting | bytes 16777216

commit v5 on v3

--- a/solution.py
+++ b/solution.py
@@ -457,7 +457,7 @@
                 wait(out_part(r, p, q), sem.at[r, q - 1, p])
 
     def relay_second(r):
-        for wave in waves[1:]:
+        for wave in waves[1:-1]:
             handed_second(r, g2_recv, wave)
             hand_out(r, hand_second, wave)
 
@@ -467,11 +467,10 @@
         "add": add_second,
         "hand": relay_second,
     }
-    pair = range(min(2, chunks))
-    order = [(act, r) for act in ("beta", "relay", "add", "hand") for r in pair]
+    order = [(act, r) for r in range(min(2, chunks)) for act in ("beta", "relay")]
+    order += [(act, r) for act in ("add", "hand") for r in range(min(2, chunks))]
     for r in range(2, chunks):
-        at = len(order) - 1
-        order.insert(at, ("beta", r))
+        order.insert(len(order) - (r == 2), ("beta", r))
         order += [(act, r) for act in ("relay", "add", "hand")]
 
     @loop(len(order))
@@ -486,6 +485,7 @@
                 act(r)
 
     for r in range(chunks):
+        handed_second(r, g2_recv, waves[-1])
         handed_second(r, g2_send, range(1, op_size))
         wait(vq.at[pl.ds(r * block, block)], o_sem.at[r])
         wait(wrecv.at[r], w_send.at[r])

time: 505 us -> 491 us (0.972)
  Pallas kernels: 496 us -> 482 us
    pallas_call x1, Pallas kernels: 496 us -> 482 us  [per_device(): pl.pallas_call(functools.partial(body, shards, op_size, slots, block, chu...]
where the time goes in v5:
time: 491 us
  Pallas kernels  482 us (98%)
  local copies, waits for them, and re-layouts  9.21 us (2%)
    pallas_call x1, Pallas kernels, per_device(): pl.pallas_call(functools.partial(body, shards, op_size, slots, block, chu...  482 us

profile of v5, /device:TPU:8, one launch (start us, length us, event | category | flops | bytes accessed | tf_op | source)
XLA Modules:
  0.0 491.2 jit_solution(9534835153526862682)
XLA Ops:
  0.0 0.8 copy.5
  0.8 0.7 reshape_squeeze.3.cols_ref
  1.4 482.0 %shard_map.46 = f32[512,4096]{1,0:T(8,128)} custom-call(s32[192]{0:T(256)} %reshape_squeeze.3.cols_ref, bf16[32,6,128,128]{3,2,1,0:T(8,128)(2,1)} %bitcast.1, f32[512,4096]{1,0:T(8,128)} %v_hbm.1, f32[512,4096]{1,0:T(8,128)} %p_hbm.1), custom_call_target="tpu_custom_call" | custom-call | flops 25769803776 | bytes 67108864 | tf_op jit(solution)/shard_map/pallas_call | solution.py:510
  483.4 7.8 %copy.7 = f32[512,4096]{1,0:T(8,128)} copy(f32[512,4096]{1,0:T(8,128)} %shard_map.46) | data formatting | bytes 16777216
